TPU v7x, 32 devices: a whole 2x2x4 slice. The times are simulated.
32 devices in a mesh: replica: 8 (over z, x), shard: 4 (over y, core).
Axes of the slice: x: 2, y: 2, z: 4, core: 2. Of those that a mesh axis runs over, the one named last changes fastest.
Arguments:
- hidden_in: bfloat16 [4096, 768], P(('replica', 'shard')), may hold values from -6 to 6
- out_cot: bfloat16 [4096, 768], P(('replica', 'shard')), may hold values from -6 to 6
- pre_gain: float32 [2, 768], replicated, may hold values from 0.5 to 1.5
- in_weight: bfloat16 [2, 768, 3352], P(None, 'shard'), may hold values from -0.21875 to 0.21875
- conv_weight: float32 [2, 4, 1792], replicated, may hold values from -2.4 to 2.4
- conv_bias: float32 [2, 1792], replicated, may hold values from -0.5 to 0.5
- dt_bias: float32 [2, 24], replicated, may hold values from -6 to -2
- a_log: float32 [2, 24], replicated, may hold values from -1.2 to 2
- skip: float32 [2, 24], replicated, may hold values from 0.5 to 1.5
- norm_gain: float32 [2, 1536], replicated, may hold values from 0.5 to 1.5
- out_weight: bfloat16 [2, 1536, 768], P(None, 'shard'), may hold values from -0.15625 to 0.15625
Outputs:
- block_out: bfloat16 [4096, 768], P(('replica', 'shard'))
- grad_in: float32 [4096, 768], P(('replica', 'shard'))
- grad_pre_gain: float32 [2, 768], replicated
- grad_in_weight: float32 [2, 768, 3352], P(None, 'shard')
- grad_conv_weight: float32 [2, 4, 1792], replicated
- grad_conv_bias: float32 [2, 1792], replicated
- grad_dt_bias: float32 [2, 24], replicated
- grad_a_log: float32 [2, 24], replicated
- grad_skip: float32 [2, 24], replicated
- grad_norm_gain: float32 [2, 1536], replicated
- grad_out_weight: float32 [2, 1536, 768], P(None, 'shard')
All inputs are finite; a program needn't handle non-finite values.
Results may differ from a plain program's by a relative error of at most 0.014.
Values may be sent and summed in bfloat16 or wider, within the bound.
A program may use at most 192 MiB of HBM per device.

v0:
```python
import jax
import jax.numpy as jnp
from jax import lax
from jax.sharding import PartitionSpec as P

DI = 1536
HEADS = 24
HEAD_DIM = 64
STATE = 128
CONV = 4
SPAN = 128
EPS = 1e-05
EXACT = lax.Precision.HIGHEST


def from_behind(value, axis, steps):
    count = lax.axis_size(axis)
    initial, last = (max(0, -steps), min(count, count - steps))
    return lax.ppermute(value, axis, [(source, source + steps) for source in range(initial, last)])


def carried_in(array, axis, combine, identity):
    length, position = (lax.axis_size(axis), lax.axis_index(axis))
    everything = jax.tree.map(lambda part: lax.all_gather(part, axis), array)
    start = jax.tree.map(
        lambda part, zero: jnp.broadcast_to(jnp.asarray(zero, part.dtype), part.shape),
        array,
        identity,
    )

    def turn(k, before):
        reached = k < position
        new = combine(before, jax.tree.map(lambda part: part[k], everything))
        return jax.tree.map(lambda a, b: jnp.where(reached, a, b), new, before)

    return lax.fori_loop(0, length, turn, start)


def entering_2(array, axis, join, neutral):
    count = lax.axis_size(axis)
    place = lax.axis_index(axis)
    ahead = count - 1 - place
    gathered = jax.tree.map(
        lambda a, kind: lax.all_gather(a.astype(kind), axis),
        array,
        jax.tree.map(lambda a: jnp.bfloat16 if a.dtype == jnp.float32 else a.dtype, array),
    )
    state = jax.tree.map(lambda a, e: jnp.zeros_like(a) + jnp.asarray(e, a.dtype), array, neutral)

    def one(turn, state):
        source = count - 1 - turn
        return join(
            state,
            jax.tree.map(
                lambda a, own: lax.dynamic_index_in_dim(a, source, 0, False).astype(own.dtype),
                gathered,
                array,
            ),
        )

    return lax.fori_loop(0, ahead, one, state)


def rms_scale(residual, gain):
    mean_sq = jnp.mean(residual * residual, axis=-1, keepdims=True)
    return residual * lax.rsqrt(mean_sq + EPS) * gain


def compose(earlier, later):
    return (earlier[0] * later[0], later[1] + later[0][..., None, None] * earlier[1])


def unpack(projected, rim_rows):
    channels = DI + 2 * STATE
    xbc_ext = jnp.concatenate([rim_rows, projected[:, DI : DI + channels]], axis=0).astype(
        jnp.float32
    )
    return (
        xbc_ext,
        projected[:, DI + channels :].astype(jnp.float32),
        projected[:, :DI].astype(jnp.float32),
    )


def prepare(xbc_ext, dt_raw, conv_w, conv_b, dt_shift, a_log):
    length = xbc_ext.shape[0] - (CONV - 1)
    conv_out = conv_b + conv_w[0] * xbc_ext[0:length]
    for offset in range(1, CONV):
        conv_out = conv_out + conv_w[offset] * xbc_ext[offset : offset + length]
    activated = jax.nn.silu(conv_out)
    blocks = length // SPAN
    x_heads = activated[:, :DI].reshape(blocks, SPAN, HEADS, HEAD_DIM)
    write_proj = activated[:, DI : DI + STATE].reshape(blocks, SPAN, STATE)
    read_proj = activated[:, DI + STATE :].reshape(blocks, SPAN, STATE)
    step_size = jax.nn.softplus(dt_raw + dt_shift)
    decay_rate = -jnp.exp(a_log)
    log_decay = jnp.cumsum((step_size * decay_rate).reshape(blocks, SPAN, HEADS), axis=1)
    return (x_heads, write_proj, read_proj, step_size.reshape(blocks, SPAN, HEADS), log_decay)


def states(x_heads, write_proj, step_size, log_decay):
    to_end = jnp.exp(log_decay[:, -1:, :] - log_decay) * step_size
    weighted = x_heads * to_end[..., None]
    span_sum = jnp.einsum("cshp,csn->chpn", weighted, write_proj, precision=EXACT)
    span_decay = jnp.exp(log_decay[:, -1, :])

    def fold(carry, item):
        return (compose(carry, item), None)

    begin = (jnp.ones_like(span_decay[0]), jnp.zeros_like(span_sum[0]))
    total, _ = lax.scan(fold, begin, (span_decay, span_sum))
    return (total[1], total[0], span_sum, span_decay)


def outputs(
    x_heads,
    write_proj,
    read_proj,
    step_size,
    log_decay,
    span_sum,
    span_decay,
    entering,
    zgate,
    skip_gain,
    norm_gain,
):

    def advance(carry, item):
        return (item[1] + item[0][:, None, None] * carry, carry)

    _, before = lax.scan(advance, entering, (span_decay, span_sum))
    scores = jnp.einsum("ctn,csn->cts", read_proj, write_proj, precision=EXACT)
    decay_heads = jnp.swapaxes(log_decay, 1, 2)
    step_heads = jnp.swapaxes(step_size, 1, 2)
    gap = decay_heads[:, :, :, None] - decay_heads[:, :, None, :]
    causal = (jnp.arange(SPAN)[:, None] >= jnp.arange(SPAN)[None, :])[None, None, :, :]
    mixing = (
        jnp.exp(jnp.where(causal, gap, -jnp.inf))
        * scores[:, None, :, :]
        * step_heads[:, :, None, :]
    )
    inside = jnp.einsum("chts,cshp->cthp", mixing, x_heads, precision=EXACT)
    carried = (
        jnp.einsum("ctn,chpn->cthp", read_proj, before, precision=EXACT)
        * jnp.exp(log_decay)[..., None]
    )
    mixed = inside + carried + skip_gain[:, None] * x_heads
    flat_rows = mixed.reshape(-1, HEADS * HEAD_DIM)
    return rms_scale(flat_rows * jax.nn.silu(zgate), norm_gain)


def inner_rows(left, right):
    return lax.dot_general(
        left, right, (((0,), (0,)), ((), ())), preferred_element_type=jnp.float32
    )


def outer_cols(left, right):
    return lax.dot_general(
        left, right, (((1,), (1,)), ((), ())), preferred_element_type=jnp.float32
    )


def shards(
    hidden_in,
    out_cot,
    pre_gain,
    in_weight,
    conv_weight,
    conv_bias,
    dt_bias,
    a_log,
    skip,
    norm_gain,
    out_weight,
):
    layer_count = in_weight.shape[0]
    rim_width = CONV - 1
    channels = DI + 2 * STATE
    residual = hidden_in.astype(jnp.float32)
    token_rows = residual.shape[0]
    in_rows = in_weight.shape[1]
    out_rows = out_weight.shape[1]
    saved = []
    for section_no in range(layer_count):
        normed = rms_scale(residual, pre_gain[section_no]).astype(jnp.bfloat16)

        def add_in(total, piece, start, normed=normed):
            return jnp.dot(normed, piece, preferred_element_type=jnp.float32)

        projected = add_in(
            jnp.zeros((token_rows, in_weight.shape[2]), jnp.float32),
            lax.all_gather(in_weight[section_no], "shard", axis=0, tiled=True),
            jnp.int32(0),
        )
        projected = projected.astype(jnp.bfloat16)
        rim_rows = from_behind(projected[token_rows - rim_width :, DI : DI + channels], "shard", 1)
        xbc_ext, dt_raw, zgate = unpack(projected, rim_rows)
        pieces = prepare(
            xbc_ext,
            dt_raw,
            conv_weight[section_no],
            conv_bias[section_no],
            dt_bias[section_no],
            a_log[section_no],
        )
        st_tot, dec_tot, span_sum, span_decay = states(pieces[0], pieces[1], pieces[3], pieces[4])
        entering = carried_in(
            (dec_tot, st_tot), "shard", compose, (jnp.ones_like(dec_tot), jnp.zeros_like(st_tot))
        )[1]
        gated_out = outputs(
            pieces[0],
            pieces[1],
            pieces[2],
            pieces[3],
            pieces[4],
            span_sum,
            span_decay,
            entering,
            zgate,
            skip[section_no],
            norm_gain[section_no],
        ).astype(jnp.bfloat16)

        def add_out(total, piece, start, gated_out=gated_out):
            return jnp.dot(gated_out, piece, preferred_element_type=jnp.float32)

        mixed = add_out(
            jnp.zeros((token_rows, out_weight.shape[2]), jnp.float32),
            lax.all_gather(out_weight[section_no], "shard", axis=0, tiled=True),
            jnp.int32(0),
        )
        saved.append((residual, normed, projected, rim_rows, entering, gated_out))
        residual = residual + mixed
    block_out = residual.astype(jnp.bfloat16)
    cotangent = out_cot.astype(jnp.float32)
    big_in = [None] * layer_count
    big_out = [None] * layer_count
    small = [None] * layer_count
    for section_no in reversed(range(layer_count)):
        residual_in, normed, projected, rim_rows, entering, gated_out = saved[section_no]
        cot_bf = cotangent.astype(jnp.bfloat16)

        def out_term(start, count, gated_out=gated_out, cot_bf=cot_bf):
            return inner_rows(gated_out, cot_bf)

        grad_out_w = lax.psum_scatter(
            out_term(jnp.int32(0), lax.axis_size("shard") * out_rows).astype(jnp.bfloat16),
            "shard",
            scatter_dimension=0,
            tiled=True,
        ).astype(jnp.float32)

        def back_out(piece, start, cot_bf=cot_bf):
            return outer_cols(cot_bf, piece)

        grad_gated = back_out(
            lax.all_gather(out_weight[section_no], "shard", axis=0, tiled=True), jnp.int32(0)
        )
        xbc_ext, dt_raw, zgate = unpack(projected, rim_rows)
        pieces, prep_back = jax.vjp(
            prepare,
            xbc_ext,
            dt_raw,
            conv_weight[section_no],
            conv_bias[section_no],
            dt_bias[section_no],
            a_log[section_no],
        )
        stats, state_back = jax.vjp(states, pieces[0], pieces[1], pieces[3], pieces[4])
        _, out_back = jax.vjp(
            outputs,
            pieces[0],
            pieces[1],
            pieces[2],
            pieces[3],
            pieces[4],
            stats[2],
            stats[3],
            entering,
            zgate,
            skip[section_no],
            norm_gain[section_no],
        )
        back_out_g = out_back(grad_gated)
        later_grad = entering_2(
            (stats[1], back_out_g[7]),
            "shard",
            compose,
            (jnp.ones_like(stats[1]), jnp.zeros_like(back_out_g[7])),
        )[1]
        grad_dec = jnp.sum(later_grad * entering, axis=(1, 2))
        from_state = state_back((later_grad, grad_dec, back_out_g[5], back_out_g[6]))
        from_prep = prep_back(
            (
                back_out_g[0] + from_state[0],
                back_out_g[1] + from_state[1],
                back_out_g[2],
                back_out_g[3] + from_state[2],
                back_out_g[4] + from_state[3],
            )
        )
        grad_ext = from_prep[0]
        returned = from_behind(grad_ext[:rim_width], "shard", -1)
        grad_own = grad_ext[rim_width:].at[token_rows - rim_width :].add(returned)
        grad_proj = jnp.concatenate([back_out_g[8], grad_own, from_prep[1]], axis=1).astype(
            jnp.bfloat16
        )

        def in_term(start, count, normed=normed, grad_proj=grad_proj):
            return inner_rows(normed, grad_proj)

        grad_in_w = lax.psum_scatter(
            in_term(jnp.int32(0), lax.axis_size("shard") * in_rows).astype(jnp.bfloat16),
            "shard",
            scatter_dimension=0,
            tiled=True,
        ).astype(jnp.float32)

        def back_in(piece, start, grad_proj=grad_proj):
            return outer_cols(grad_proj, piece)

        grad_normed = back_in(
            lax.all_gather(in_weight[section_no], "shard", axis=0, tiled=True), jnp.int32(0)
        )
        _, norm_back = jax.vjp(rms_scale, residual_in, pre_gain[section_no])
        grad_res, grad_pre = norm_back(grad_normed)
        cotangent = cotangent + grad_res
        small[section_no] = (
            grad_pre,
            from_prep[2],
            from_prep[3],
            from_prep[4],
            from_prep[5],
            back_out_g[9],
            back_out_g[10],
        )
        grad_in_w, grad_out_w = lax.psum((grad_in_w, grad_out_w), "replica")
        big_in[section_no] = grad_in_w
        big_out[section_no] = grad_out_w
    stacked_in = jnp.stack(big_in)
    stacked_out = jnp.stack(big_out)
    columns = [
        jnp.stack([small[number][member] for number in range(layer_count)]) for member in range(7)
    ]
    summed = lax.psum(
        (columns[0], columns[1], columns[2], columns[3], columns[4], columns[5], columns[6]),
        ("replica", "shard"),
    )
    return (
        block_out,
        cotangent,
        summed[0],
        stacked_in,
        summed[1],
        summed[2],
        summed[3],
        summed[4],
        summed[5],
        summed[6],
        stacked_out,
    )


def solution(mesh):
    return jax.shard_map(
        shards,
        mesh=mesh,
        in_specs=(
            P(("replica", "shard"), None),
            P(("replica", "shard"), None),
            P(),
            P(None, "shard", None),
            P(),
            P(),
            P(),
            P(),
            P(),
            P(),
            P(None, "shard", None),
        ),
        out_specs=(
            P(("replica", "shard"), None),
            P(("replica", "shard"), None),
            P(),
            P(None, "shard", None),
            P(),
            P(),
            P(),
            P(),
            P(),
            P(),
            P(None, "shard", None),
        ),
        check_vma=False,
    )
```

profile of v0, /device:TPU:8, one launch (start us, length us, event | category | flops | bytes accessed | tf_op | source)
XLA Modules:
  0.0 944.2 jit_solution(16295703544789042874)
XLA Ops:
  7.3 3.4 fusion.225
  13.9 38.8 %all-gather.21.cloned.1.call-done = bf16[1,768,3352]{2,1,0:T(8,128)(2,1)} async-done(((bf16[1,192,3352]{2,1,0:T(8,128)(2,1)}), bf16[1,768,3352]{2,1,0:T(8,128)(2,1)}) %all-gather.21.cloned.1.call-update) | async-done | bytes 5148688 | tf_op jit(solution)/shard_map/all_gather | solution.py:194
  52.8 3.4 fusion.10
  74.3 5.4 all-gather.2
  81.3 17.1 %all-gather.23.cloned.1.call-done = f32[96,64,128]{2,1,0:T(8,128)} async-done(((f32[24,64,128]{2,1,0:T(8,128)}), f32[96,64,128]{2,1,0:T(8,128)}) %all-gather.23.cloned.1.call-update) | async-done | bytes 3145744 | tf_op jit(solution)/shard_map/all_gather | solution.py:24
  98.4 10.1 %while.40 = (s32[]{:T(128)}, f32[24,64,128]{2,1,0:T(8,128)S(1)}, s32[]{:T(128)}, f32[4,24,64,128]{3,2,1,0:T(8,128)}, f32[4,24]{1,0:T(4,128)}, /*index=5*/s32[]{:T(128)}, s32[]{:T(128)}) while((s32[]{:T(128)}, f32[24,64,128]{2,1,0:T(8,128)S(1)}, s32[]{:T(128)}, f32[4,24,64,128]{3,2,1,0:T(8,128)}, f32[4,24]{1,0:T(4,128)}, ...), condition=%wide.region_3.4_spmd.clone, body=%wide.region_2.3_spmd.clone.sunk | while | flops 786436 | bytes 2359697 | solution.py:36
  109.4 4.1 fusion.69
  117.8 6.2 all-gather.25.cloned.1.call-done
  126.4 40.4 %all-gather.27.cloned.1.call-done = bf16[1,768,3352]{2,1,0:T(8,128)(2,1)} async-done(((bf16[1,192,3352]{2,1,0:T(8,128)(2,1)}), bf16[1,768,3352]{2,1,0:T(8,128)(2,1)}) %all-gather.27.cloned.1.call-update) | async-done | bytes 5148688 | tf_op jit(solution)/shard_map/all_gather | solution.py:194
  166.8 3.5 fusion.13
  182.8 2.6 convolution_add_fusion.2
  194.6 5.8 all-gather.6
  204.5 10.4 %all-gather.29.cloned.1.call-done = f32[96,64,128]{2,1,0:T(8,128)} async-done(((f32[24,64,128]{2,1,0:T(8,128)}), f32[96,64,128]{2,1,0:T(8,128)}) %all-gather.29.cloned.1.call-update) | async-done | bytes 3145744 | tf_op jit(solution)/shard_map/all_gather | solution.py:24
  214.9 10.2 %while.41 = (s32[]{:T(128)}, f32[24,64,128]{2,1,0:T(8,128)S(1)}, s32[]{:T(128)}, f32[4,24,64,128]{3,2,1,0:T(8,128)}, f32[4,24]{1,0:T(4,128)}, /*index=5*/s32[]{:T(128)}, s32[]{:T(128)}) while((s32[]{:T(128)}, f32[24,64,128]{2,1,0:T(8,128)S(1)}, s32[]{:T(128)}, f32[4,24,64,128]{3,2,1,0:T(8,128)}, f32[4,24]{1,0:T(4,128)}, ...), condition=%wide.region_8.9_spmd.clone, body=%wide.region_7.8_spmd.clone.sunk | while | flops 786436 | bytes 2359697 | solution.py:36
  227.2 4.1 fusion.57
  237.1 3.3 all-gather.31.cloned.1.call-done
  240.4 3.6 multiply_reduce_fusion.12
  250.2 2.7 fusion.72
  257.0 5.4 all-gather.9
  268.8 5.7 fusion.88
  284.9 6.2 while.38
  291.2 2.7 multiply_reduce_fusion.26
  294.8 2.8 fusion.51
  299.9 2.7 fusion.86
  319.7 5.1 multiply_reduce_fusion.30
  327.6 3.0 multiply_reduce_fusion.15
  334.9 2.7 fusion.73
  337.7 2.9 convolution_convert_fusion.2
  341.3 3.4 convolution_convert_fusion.3
  345.9 5.0 convolution_convert_fusion
  351.6 5.5 all-gather.11
  360.8 4.9 fusion.90
  369.6 2.6 convolution_bitcast_fusion.3
  374.0 3.7 while.39
  377.7 3.0 multiply_reduce_fusion.20
  380.9 4.3 fusion.63
  387.5 2.7 fusion.84
  402.9 4.1 convolution_convert_fusion.1
  409.3 20.1 %reduce-scatter.9.cloned.1.call-done = bf16[384,768]{1,0:T(8,128)(2,1)} async-done(((bf16[1536,768]{1,0:T(8,128)(2,1)}), bf16[384,768]{1,0:T(8,128)(2,1)}) %reduce-scatter.9.cloned.1.call-update) | async-done | bytes 589840 | tf_op jit(solution)/shard_map/reduce_scatter | solution.py:248
  431.6 52.8 %reduce-scatter.7.cloned.1.call-done = bf16[192,3352]{1,0:T(8,128)(2,1)} async-done(((bf16[768,3352]{1,0:T(8,128)(2,1)}), bf16[192,3352]{1,0:T(8,128)(2,1)}) %reduce-scatter.7.cloned.1.call-update) | async-done | bytes 1287184 | tf_op jit(solution)/shard_map/reduce_scatter | solution.py:314
  484.4 3.0 bitcast_convert_fusion.2
  487.4 51.2 %reduce-scatter.5.cloned.1.call-done = bf16[192,3352]{1,0:T(8,128)(2,1)} async-done(((bf16[768,3352]{1,0:T(8,128)(2,1)}), bf16[192,3352]{1,0:T(8,128)(2,1)}) %reduce-scatter.5.cloned.1.call-update) | async-done | bytes 1287184 | tf_op jit(solution)/shard_map/reduce_scatter | solution.py:314
  538.6 3.1 bitcast_convert_fusion.3
  542.8 3.0 fusion.80
  550.0 4.7 fusion.136
  556.2 236.5 %all-reduce.33.cloned.1.call-done = (f32[1,192,3352]{2,1,0:T(8,128)}, f32[1,192,3352]{2,1,0:T(8,128)}, f32[1,384,768]{2,1,0:T(8,128)}, f32[1,384,768]{2,1,0:T(8,128)}) async-done(((f32[1,192,3352]{2,1,0:T(8,128)}, f32[1,192,3352]{2,1,0:T(8,128)}, f32[1,384,768]{2,1,0:T(8,128)}, f32[1,384,768]{2,1,0:T(8,128)}), (f32[1,192,3352]{2,1,0:T(8,128)}, f32[1,192,3352]{2,1,0:T(8,128)}, f32[1,384,768]{2,1,0:T(8,128)}, ...) | async-done | bytes 7507984 | tf_op jit(solution)/shard_map/psum | solution.py:339
  792.7 5.4 pad_maximum_fusion
  799.6 128.6 %all-reduce.31.cloned.1.call-done = (f32[2,768]{1,0:T(2,128)}, f32[2,4,1792]{2,1,0:T(4,128)}, f32[2,1792]{1,0:T(2,128)}, f32[2,24]{1,0:T(2,128)}, f32[2,24]{1,0:...) async-done(((f32[2,768]{1,0:T(2,128)}, f32[2,4,1792]{2,1,0:T(4,128)}, f32[2,1792]{1,0:T(2,128)}, f32[2,24]{1,0:T(2,128)}, f32[2,24]{1,0:T(2,128)}, ...) | async-done | bytes 90704 | tf_op jit(solution)/shard_map/psum | solution.py:347
  (600 shorter events, 195.1 us)
Async XLA Ops:
  7.2 45.6 %all-gather.21.cloned.1.call-start = ((), (), s32[]{:S(2)}) async-start(), calls=%async_computation.8 | async-start | bytes 6635520 | tf_op jit(solution)/shard_map/all_gather | solution.py:194
  10.7 87.7 %all-gather.23.cloned.1.call-start = ((), (), s32[]{:S(2)}) async-start(), calls=%async_computation.9 | async-start | bytes 3932160 | tf_op jit(solution)/shard_map/all_gather | solution.py:24
  11.4 44.9 %copy-start.90 = (f32[768]{0:T(1024)}, f32[768]{0:T(1024)S(1)}, u32[]{:S(2)}) copy-start(f32[768]{0:T(1024)S(1)} %get-tuple-element.724) | copy-start | bytes 9220
  12.7 48.4 %copy-start.103 = (f32[1792]{0:T(1024)}, f32[1792]{0:T(1024)S(1)}, u32[]{:S(2)}) copy-start(f32[1792]{0:T(1024)S(1)} %get-tuple-element.713) | copy-start | bytes 21508
  12.7 48.4 %copy-start.105 = (f32[1792]{0:T(1024)}, f32[1792]{0:T(1024)S(1)}, u32[]{:S(2)}) copy-start(f32[1792]{0:T(1024)S(1)} %get-tuple-element.714) | copy-start | bytes 21508
  12.7 48.4 %copy-start.107 = (f32[1792]{0:T(1024)}, f32[1792]{0:T(1024)S(1)}, u32[]{:S(2)}) copy-start(f32[1792]{0:T(1024)S(1)} %get-tuple-element.715) | copy-start | bytes 21508
  13.4 42.8 %copy-start.144 = (f32[128]{0:T(128)}, f32[128]{0:T(128)S(1)}, u32[]{:S(2)}) copy-start(f32[128]{0:T(128)S(1)} %fusion.199) | copy-start | bytes 1540
  13.9 42.3 %copy-start.154 = (f32[24]{0:T(128)}, f32[24]{0:T(128)S(1)}, u32[]{:S(2)}) copy-start(f32[24]{0:T(128)S(1)} %get-tuple-element.833) | copy-start | bytes 292
  13.9 43.2 %copy-start.134 = (f32[24]{0:T(128)}, f32[24]{0:T(128)S(1)}, u32[]{:S(2)}) copy-start(f32[24]{0:T(128)S(1)} %get-tuple-element.844) | copy-start | bytes 292
  56.5 16.4 %copy-start.54 = (f32[1,128,24]{2,1,0:T(8,128)}, f32[1,128,24]{2,1,0:T(8,128)S(1)}, u32[]{:S(2)}) copy-start(f32[1,128,24]{2,1,0:T(8,128)S(1)} %reduce_window_sum.47) | copy-start | bytes 36868
  57.8 3.1 collective-permute-start
  63.4 45.1 %copy-start.25 = (f32[128,1792]{1,0:T(8,128)}, f32[128,1792]{1,0:T(8,128)S(1)}, u32[]{:S(2)}) copy-start(f32[128,1792]{1,0:T(8,128)S(1)} %get-tuple-element.792) | copy-start | bytes 2752516
  68.0 56.1 %all-gather.25.cloned.1.call-start = ((), (), s32[]{:S(2)}) async-start(), calls=%async_computation.10 | async-start | bytes 2949120 | tf_op jit(solution)/shard_map/all_gather | solution.py:231
  70.4 96.4 %all-gather.27.cloned.1.call-start = ((), (), s32[]{:S(2)}) async-start(), calls=%async_computation.11 | async-start | bytes 6635520 | tf_op jit(solution)/shard_map/all_gather | solution.py:194
  71.0 143.9 %all-gather.29.cloned.1.call-start = ((), (), s32[]{:S(2)}) async-start(), calls=%async_computation.12 | async-start | bytes 3932160 | tf_op jit(solution)/shard_map/all_gather | solution.py:24
  81.0 28.3 %copy-start.18 = (f32[128,1536]{0,1:T(8,128)}, f32[128,1536]{0,1:T(8,128)S(1)}, u32[]{:S(2)}) copy-start(f32[128,1536]{0,1:T(8,128)S(1)} %copy.347) | copy-start | bytes 2359300
  81.3 28.0 %copy-start.66 = (f32[128,128]{1,0:T(8,128)}, f32[128,128]{1,0:T(8,128)S(1)}, u32[]{:S(2)}) copy-start(f32[128,128]{1,0:T(8,128)S(1)} %fusion.191) | copy-start | bytes 196612
  113.5 10.5 %copy-start.45 = (bf16[128,768]{1,0:T(8,128)(2,1)S(1)}, bf16[128,768]{1,0:T(8,128)(2,1)}, u32[]{:S(2)}) copy-start(bf16[128,768]{1,0:T(8,128)(2,1)} %param.24) | copy-start | bytes 589828
  115.0 9.0 copy-start.34
  116.7 9.7 %copy-start.4 = (f32[128,1536]{1,0:T(8,128)}, f32[128,1536]{1,0:T(8,128)S(1)}, u32[]{:S(2)}) copy-start(f32[128,1536]{1,0:T(8,128)S(1)} %get-tuple-element.791) | copy-start | bytes 2359300
  124.0 42.8 %copy-start.87 = (f32[768]{0:T(1024)S(1)}, f32[768]{0:T(1024)}, u32[]{:S(2)}) copy-start(f32[768]{0:T(1024)} %get-tuple-element.723) | copy-start | bytes 9220
  126.4 40.5 %copy-start.179 = (f32[128]{0:T(128)}, f32[128]{0:T(128)S(1)}, u32[]{:S(2)}) copy-start(f32[128]{0:T(128)S(1)} %get-tuple-element.834) | copy-start | bytes 1540
  126.4 43.9 %copy-start.20 = (f32[128,768]{1,0:T(8,128)}, f32[128,768]{1,0:T(8,128)S(1)}, u32[]{:S(2)}) copy-start(f32[128,768]{1,0:T(8,128)S(1)} %get-tuple-element.835) | copy-start | bytes 1179652
  126.4 43.9 %copy-start.146 = (f32[128]{0:T(128)}, f32[128]{0:T(128)S(1)}, u32[]{:S(2)}) copy-start(f32[128]{0:T(128)S(1)} %fusion.201) | copy-start | bytes 1540
  171.5 5.4 copy-start.56
  174.1 4.2 collective-permute-start.1
  185.4 55.0 %all-gather.31.cloned.1.call-start = ((), (), s32[]{:S(2)}) async-start(), calls=%async_computation.13 | async-start | bytes 2949120 | tf_op jit(solution)/shard_map/all_gather | solution.py:231
  186.0 98.8 %all-gather.33.cloned.1.call-start = ((), (), s32[]{:S(2)}) async-start(), calls=%async_computation.14 | async-start | bytes 1966080 | tf_op jit(solution)/shard_map/all_gather | solution.py:44
  225.1 55.5 %copy-start = (f32[24,64,128]{2,1,0:T(8,128)}, f32[24,64,128]{2,1,0:T(8,128)S(1)}, u32[]{:S(2)}) copy-start(f32[24,64,128]{2,1,0:T(8,128)S(1)} %get-tuple-element.636) | copy-start | bytes 2359300
  253.0 120.9 %all-gather.35.cloned.1.call-start = ((), (), s32[]{:S(2)}) async-start(), calls=%async_computation.15 | async-start | bytes 1966080 | tf_op jit(solution)/shard_map/all_gather | solution.py:44
  306.8 6.7 copy-start.76
  306.8 6.7 copy-start.157
  308.4 8.1 collective-permute-start.2
  319.7 5.4 copy-start.29
  319.7 5.4 copy-start.85
  319.7 5.4 copy-start.149
  337.6 69.5 %reduce-scatter.11.cloned.1.call-start = ((), (), s32[]{:S(2)}) async-start(), calls=%async_computation.7 | async-start | bytes 2949120 | tf_op jit(solution)/shard_map/reduce_scatter | solution.py:248
  340.6 88.8 %reduce-scatter.9.cloned.1.call-start = ((), (), s32[]{:S(2)}) async-start(), calls=%async_computation.6 | async-start | bytes 2949120 | tf_op jit(solution)/shard_map/reduce_scatter | solution.py:248
  344.7 139.6 %reduce-scatter.7.cloned.1.call-start = ((), (), s32[]{:S(2)}) async-start(), calls=%async_computation.5 | async-start | bytes 6635520 | tf_op jit(solution)/shard_map/reduce_scatter | solution.py:314
  351.0 187.6 %reduce-scatter.5.cloned.1.call-start = ((), (), s32[]{:S(2)}) async-start(), calls=%async_computation.4 | async-start | bytes 6635520 | tf_op jit(solution)/shard_map/reduce_scatter | solution.py:314
  358.5 7.2 copy-start.16
  393.6 8.2 collective-permute-start.3
  407.0 385.6 %all-reduce.33.cloned.1.call-start = ((), (), s32[]{:S(2)}) async-start(), calls=%async_computation.17 | async-start | bytes 15335424 | tf_op jit(solution)/shard_map/psum | solution.py:339
  541.7 386.5 %all-reduce.31.cloned.1.call-start = ((), (), s32[]{:S(2)}) async-start(), calls=%async_computation.16 | async-start | bytes 186368 | tf_op jit(solution)/shard_map/psum | solution.py:347
  550.0 5.3 copy-start.176
  550.0 5.3 copy-start.40
  792.7 5.4 copy-start.64
  792.7 5.4 copy-start.65
  (154 other events, 393.8 us)
Sparse Core Ops, SparseCore 0:
  10.8 41.9 all-gather.20
  68.1 30.2 all-gather.22
  100.0 24.0 all-gather.24
  126.0 40.7 all-gather.26
  185.5 29.3 all-gather.28
  216.3 24.0 all-gather.30
  253.1 19.6 all-gather.32
  337.8 20.4 all-gather.34
  361.3 32.8 reduce-scatter.10
  396.6 32.8 reduce-scatter.8
  432.5 51.7 reduce-scatter.6
  486.8 51.7 reduce-scatter.4
  544.3 248.2 all-reduce.32
  800.1 128.0 all-reduce.30
where the time goes:
time: 956 us; the launch traced here: 944 us
  waiting for transfers between devices  607 us (63%)
  matrix products  106 us (11%)
  local copies, waits for them, and re-layouts  92.1 us (10%)
  other arithmetic  91.7 us (10%)
  blocking collectives  22.1 us (2%)
  between operations  16.5 us (2%)
    psum x1, waiting for transfers between devices, shards(): grad_in_w, grad_out_w = lax.psum((grad_in_w, grad_out_w), 'replica')  236 us
    psum x1, waiting for transfers between devices, shards(): lax.psum((columns[0], columns[1], columns[2], columns[3], columns[4], col...  129 us
    reduce_scatter x2, waiting for transfers between devices, shards(): lax.psum_scatter(in_term(jnp.int32(0), lax.axis_size('shard') * in_rows)....  104 us
    all_gather x2, waiting for transfers between devices, shards(): lax.all_gather(in_weight[section_no], 'shard', axis=0, tiled=True)  79.3 us
    all_gather x2, waiting for transfers between devices, carried_in(): everything = jax.tree.map(lambda part: lax.all_gather(part, axis), array)  27.5 us
    dot_general x6, matrix products, outputs(): inside = jnp.einsum('chts,cshp->cthp', mixing, x_heads, precision=EXACT)  25.9 us
    unnamed x375, local copies, waits for them, and re-layouts  22.9 us
    reduce_scatter x2, waiting for transfers between devices, shards(): lax.psum_scatter(out_term(jnp.int32(0), lax.axis_size('shard') * out_rows...  20.1 us
  transfers between devices with their start and end apart: 18, of which 11 were waited for; matrix products, arithmetic and copies ran while one was open for 20% of the time, Pallas kernels for 0%

commit v1 on v0

--- a/solution.py
+++ b/solution.py
@@ -344,10 +344,8 @@
     columns = [
         jnp.stack([small[number][member] for number in range(layer_count)]) for member in range(7)
     ]
-    summed = lax.psum(
-        (columns[0], columns[1], columns[2], columns[3], columns[4], columns[5], columns[6]),
-        ("replica", "shard"),
-    )
+    arr = (columns[0], columns[1], columns[2], columns[3], columns[4], columns[5], columns[6])
+    summed = lax.psum(lax.psum(arr, axis_name="shard"), axis_name="replica")
     return (
         block_out,
         cotangent,

time: 956 us -> 935 us (0.978)
  waiting for transfers between devices: 607 us -> 583 us
    psum x1 -> x2, waiting for transfers between devices: 129 us -> 97.6 us  [shards(): summed = lax.psum(lax.psum(arr, axis_name='shard'), axis_name='replica')]
    psum x1, waiting for transfers between devices: 236 us -> 254 us  [shards(): grad_in_w, grad_out_w = lax.psum((grad_in_w, grad_out_w), 'replica')]
    reduce_scatter x2, waiting for transfers between devices: 20.1 us -> 10.2 us  [shards(): lax.psum_scatter(out_term(jnp.int32(0), lax.axis_size('shard') * out_rows...]
  transfers between devices with their start and end apart: 18 -> 19, of which waited for: 11 -> 12; matrix products, arithmetic and copies ran while one was open for 20% -> 20% of each run, Pallas kernels for 0% -> 0%
where the time goes in v1:
time: 935 us; the launch traced here: 921 us
  waiting for transfers between devices  583 us (62%)
  matrix products  106 us (11%)
  local copies, waits for them, and re-layouts  92.6 us (10%)
  other arithmetic  91.9 us (10%)
  blocking collectives  22.4 us (2%)
  between operations  16.6 us (2%)
    psum x1, waiting for transfers between devices, shards(): grad_in_w, grad_out_w = lax.psum((grad_in_w, grad_out_w), 'replica')  254 us
    reduce_scatter x2, waiting for transfers between devices, shards(): lax.psum_scatter(in_term(jnp.int32(0), lax.axis_size('shard') * in_rows)....  104 us
    psum x2, waiting for transfers between devices, shards(): summed = lax.psum(lax.psum(arr, axis_name='shard'), axis_name='replica')  97.6 us
    all_gather x2, waiting for transfers between devices, shards(): lax.all_gather(in_weight[section_no], 'shard', axis=0, tiled=True)  79.2 us
    all_gather x2, waiting for transfers between devices, carried_in(): everything = jax.tree.map(lambda part: lax.all_gather(part, axis), array)  27 us
    dot_general x6, matrix products, outputs(): inside = jnp.einsum('chts,cshp->cthp', mixing, x_heads, precision=EXACT)  26 us
    unnamed x375, local copies, waits for them, and re-layouts  23.5 us
  transfers between devices with their start and end apart: 19, of which 12 were waited for; matrix products, arithmetic and copies ran while one was open for 20% of the time, Pallas kernels for 0%

profile of v1, /device:TPU:8, one launch (start us, length us, event | category | flops | bytes accessed | tf_op | source)
XLA Modules:
  0.0 920.8 jit_solution(5300321304736337917)
XLA Ops:
  7.3 3.4 fusion.225
  13.9 38.8 %all-gather.21.cloned.1.call-done = bf16[1,768,3352]{2,1,0:T(8,128)(2,1)} async-done(((bf16[1,192,3352]{2,1,0:T(8,128)(2,1)}), bf16[1,768,3352]{2,1,0:T(8,128)(2,1)}) %all-gather.21.cloned.1.call-update) | async-done | bytes 5148688 | tf_op jit(solution)/shard_map/all_gather | solution.py:194
  52.8 3.4 fusion.10
  74.4 5.3 all-gather.2
  81.4 17.1 %all-gather.23.cloned.1.call-done = f32[96,64,128]{2,1,0:T(8,128)} async-done(((f32[24,64,128]{2,1,0:T(8,128)}), f32[96,64,128]{2,1,0:T(8,128)}) %all-gather.23.cloned.1.call-update) | async-done | bytes 3145744 | tf_op jit(solution)/shard_map/all_gather | solution.py:24
  98.4 10.1 %while.40 = (s32[]{:T(128)}, f32[24,64,128]{2,1,0:T(8,128)S(1)}, s32[]{:T(128)}, f32[4,24,64,128]{3,2,1,0:T(8,128)}, f32[4,24]{1,0:T(4,128)}, /*index=5*/s32[]{:T(128)}, s32[]{:T(128)}) while((s32[]{:T(128)}, f32[24,64,128]{2,1,0:T(8,128)S(1)}, s32[]{:T(128)}, f32[4,24,64,128]{3,2,1,0:T(8,128)}, f32[4,24]{1,0:T(4,128)}, ...), condition=%wide.region_3.4_spmd.clone, body=%wide.region_2.3_spmd.clone.sunk | while | flops 786436 | bytes 2359697 | solution.py:36
  109.5 4.1 fusion.69
  117.9 6.2 all-gather.25.cloned.1.call-done
  126.5 40.4 %all-gather.27.cloned.1.call-done = bf16[1,768,3352]{2,1,0:T(8,128)(2,1)} async-done(((bf16[1,192,3352]{2,1,0:T(8,128)(2,1)}), bf16[1,768,3352]{2,1,0:T(8,128)(2,1)}) %all-gather.27.cloned.1.call-update) | async-done | bytes 5148688 | tf_op jit(solution)/shard_map/all_gather | solution.py:194
  166.9 3.5 fusion.13
  194.7 6.2 all-gather.6
  205.0 9.9 %all-gather.29.cloned.1.call-done = f32[96,64,128]{2,1,0:T(8,128)} async-done(((f32[24,64,128]{2,1,0:T(8,128)}), f32[96,64,128]{2,1,0:T(8,128)}) %all-gather.29.cloned.1.call-update) | async-done | bytes 3145744 | tf_op jit(solution)/shard_map/all_gather | solution.py:24
  214.9 10.1 %while.41 = (s32[]{:T(128)}, f32[24,64,128]{2,1,0:T(8,128)S(1)}, s32[]{:T(128)}, f32[4,24,64,128]{3,2,1,0:T(8,128)}, f32[4,24]{1,0:T(4,128)}, /*index=5*/s32[]{:T(128)}, s32[]{:T(128)}) while((s32[]{:T(128)}, f32[24,64,128]{2,1,0:T(8,128)S(1)}, s32[]{:T(128)}, f32[4,24,64,128]{3,2,1,0:T(8,128)}, f32[4,24]{1,0:T(4,128)}, ...), condition=%wide.region_8.9_spmd.clone, body=%wide.region_7.8_spmd.clone.sunk | while | flops 786436 | bytes 2359697 | solution.py:36
  227.1 4.1 fusion.57
  237.0 3.4 all-gather.31.cloned.1.call-done
  240.4 3.6 multiply_reduce_fusion.12
  250.2 2.7 fusion.72
  257.0 5.4 all-gather.9
  268.8 5.7 fusion.88
  284.9 6.2 while.38
  291.2 2.7 multiply_reduce_fusion.26
  294.8 2.8 fusion.51
  299.9 2.7 fusion.86
  319.8 5.1 multiply_reduce_fusion.30
  327.6 3.1 multiply_reduce_fusion.15
  334.9 2.7 fusion.73
  337.7 2.9 convolution_convert_fusion.2
  341.3 3.4 convolution_convert_fusion.3
  345.9 5.0 convolution_convert_fusion
  351.6 5.4 all-gather.11
  360.8 4.9 fusion.90
  369.6 2.6 convolution_bitcast_fusion.3
  374.0 3.7 while.39
  377.8 3.0 multiply_reduce_fusion.20
  380.9 4.3 fusion.63
  387.6 2.7 fusion.84
  403.0 4.1 convolution_convert_fusion.1
  414.3 4.2 fusion.136
  419.2 10.2 %reduce-scatter.9.cloned.1.call-done = bf16[384,768]{1,0:T(8,128)(2,1)} async-done(((bf16[1536,768]{1,0:T(8,128)(2,1)}), bf16[384,768]{1,0:T(8,128)(2,1)}) %reduce-scatter.9.cloned.1.call-update) | async-done | bytes 589840 | tf_op jit(solution)/shard_map/reduce_scatter | solution.py:248
  431.6 52.8 %reduce-scatter.7.cloned.1.call-done = bf16[192,3352]{1,0:T(8,128)(2,1)} async-done(((bf16[768,3352]{1,0:T(8,128)(2,1)}), bf16[192,3352]{1,0:T(8,128)(2,1)}) %reduce-scatter.7.cloned.1.call-update) | async-done | bytes 1287184 | tf_op jit(solution)/shard_map/reduce_scatter | solution.py:314
  484.4 3.0 bitcast_convert_fusion.2
  487.4 51.2 %reduce-scatter.5.cloned.1.call-done = bf16[192,3352]{1,0:T(8,128)(2,1)} async-done(((bf16[768,3352]{1,0:T(8,128)(2,1)}), bf16[192,3352]{1,0:T(8,128)(2,1)}) %reduce-scatter.5.cloned.1.call-update) | async-done | bytes 1287184 | tf_op jit(solution)/shard_map/reduce_scatter | solution.py:314
  538.6 3.0 bitcast_convert_fusion.3
  542.6 2.9 fusion.80
  546.4 28.4 %all-reduce.37.cloned.1.call-done = (f32[2,768]{1,0:T(2,128)}, f32[2,4,1792]{2,1,0:T(4,128)}, f32[2,1792]{1,0:T(2,128)}, f32[2,24]{1,0:T(2,128)}, f32[2,24]{1,0:...) async-done(((f32[2,768]{1,0:T(2,128)}, f32[2,4,1792]{2,1,0:T(4,128)}, f32[2,1792]{1,0:T(2,128)}, f32[2,24]{1,0:T(2,128)}, f32[2,24]{1,0:T(2,128)}, ...) | async-done | bytes 90704 | tf_op jit(solution)/shard_map/psum | solution.py:348
  574.8 253.9 %all-reduce.35.cloned.1.call-done = (f32[1,192,3352]{2,1,0:T(8,128)}, f32[1,192,3352]{2,1,0:T(8,128)}, f32[1,384,768]{2,1,0:T(8,128)}, f32[1,384,768]{2,1,0:T(8,128)}) async-done(((f32[1,192,3352]{2,1,0:T(8,128)}, f32[1,192,3352]{2,1,0:T(8,128)}, f32[1,384,768]{2,1,0:T(8,128)}, f32[1,384,768]{2,1,0:T(8,128)}), (f32[1,192,3352]{2,1,0:T(8,128)}, f32[1,192,3352]{2,1,0:T(8,128)}, f32[1,384,768]{2,1,0:T(8,128)}, ...) | async-done | bytes 7507984 | tf_op jit(solution)/shard_map/psum | solution.py:339
  828.7 5.4 pad_maximum_fusion
  835.7 69.2 %all-reduce.33.cloned.1.call-done = (f32[2,768]{1,0:T(2,128)}, f32[2,4,1792]{2,1,0:T(4,128)}, f32[2,1792]{1,0:T(2,128)}, f32[2,24]{1,0:T(2,128)}, f32[2,24]{1,0:...) async-done(((f32[2,768]{1,0:T(2,128)}, f32[2,4,1792]{2,1,0:T(4,128)}, f32[2,1792]{1,0:T(2,128)}, f32[2,24]{1,0:T(2,128)}, f32[2,24]{1,0:T(2,128)}, ...) | async-done | bytes 90704 | tf_op jit(solution)/shard_map/psum | solution.py:348
  (603 shorter events, 198.5 us)
Async XLA Ops:
  7.2 45.6 %all-gather.21.cloned.1.call-start = ((), (), s32[]{:S(2)}) async-start(), calls=%async_computation.8 | async-start | bytes 6635520 | tf_op jit(solution)/shard_map/all_gather | solution.py:194
  10.7 87.7 %all-gather.23.cloned.1.call-start = ((), (), s32[]{:S(2)}) async-start(), calls=%async_computation.9 | async-start | bytes 3932160 | tf_op jit(solution)/shard_map/all_gather | solution.py:24
  11.4 44.9 %copy-start.90 = (f32[768]{0:T(1024)}, f32[768]{0:T(1024)S(1)}, u32[]{:S(2)}) copy-start(f32[768]{0:T(1024)S(1)} %get-tuple-element.724) | copy-start | bytes 9220
  12.7 48.6 %copy-start.103 = (f32[1792]{0:T(1024)}, f32[1792]{0:T(1024)S(1)}, u32[]{:S(2)}) copy-start(f32[1792]{0:T(1024)S(1)} %get-tuple-element.713) | copy-start | bytes 21508
  12.7 48.6 %copy-start.105 = (f32[1792]{0:T(1024)}, f32[1792]{0:T(1024)S(1)}, u32[]{:S(2)}) copy-start(f32[1792]{0:T(1024)S(1)} %get-tuple-element.714) | copy-start | bytes 21508
  12.7 48.6 %copy-start.107 = (f32[1792]{0:T(1024)}, f32[1792]{0:T(1024)S(1)}, u32[]{:S(2)}) copy-start(f32[1792]{0:T(1024)S(1)} %get-tuple-element.715) | copy-start | bytes 21508
  13.4 42.8 %copy-start.144 = (f32[128]{0:T(128)}, f32[128]{0:T(128)S(1)}, u32[]{:S(2)}) copy-start(f32[128]{0:T(128)S(1)} %fusion.199) | copy-start | bytes 1540
  13.9 42.3 %copy-start.154 = (f32[24]{0:T(128)}, f32[24]{0:T(128)S(1)}, u32[]{:S(2)}) copy-start(f32[24]{0:T(128)S(1)} %get-tuple-element.840) | copy-start | bytes 292
  13.9 43.2 %copy-start.134 = (f32[24]{0:T(128)}, f32[24]{0:T(128)S(1)}, u32[]{:S(2)}) copy-start(f32[24]{0:T(128)S(1)} %get-tuple-element.851) | copy-start | bytes 292
  56.5 16.5 %copy-start.54 = (f32[1,128,24]{2,1,0:T(8,128)}, f32[1,128,24]{2,1,0:T(8,128)S(1)}, u32[]{:S(2)}) copy-start(f32[1,128,24]{2,1,0:T(8,128)S(1)} %reduce_window_sum.47) | copy-start | bytes 36868
  57.8 3.2 collective-permute-start
  63.5 45.1 %copy-start.25 = (f32[128,1792]{1,0:T(8,128)}, f32[128,1792]{1,0:T(8,128)S(1)}, u32[]{:S(2)}) copy-start(f32[128,1792]{1,0:T(8,128)S(1)} %get-tuple-element.799) | copy-start | bytes 2752516
  68.1 56.0 %all-gather.25.cloned.1.call-start = ((), (), s32[]{:S(2)}) async-start(), calls=%async_computation.10 | async-start | bytes 2949120 | tf_op jit(solution)/shard_map/all_gather | solution.py:231
  70.5 96.4 %all-gather.27.cloned.1.call-start = ((), (), s32[]{:S(2)}) async-start(), calls=%async_computation.11 | async-start | bytes 6635520 | tf_op jit(solution)/shard_map/all_gather | solution.py:194
  71.1 143.8 %all-gather.29.cloned.1.call-start = ((), (), s32[]{:S(2)}) async-start(), calls=%async_computation.12 | async-start | bytes 3932160 | tf_op jit(solution)/shard_map/all_gather | solution.py:24
  81.1 28.3 %copy-start.18 = (f32[128,1536]{0,1:T(8,128)}, f32[128,1536]{0,1:T(8,128)S(1)}, u32[]{:S(2)}) copy-start(f32[128,1536]{0,1:T(8,128)S(1)} %copy.347) | copy-start | bytes 2359300
  81.3 28.1 %copy-start.66 = (f32[128,128]{1,0:T(8,128)}, f32[128,128]{1,0:T(8,128)S(1)}, u32[]{:S(2)}) copy-start(f32[128,128]{1,0:T(8,128)S(1)} %fusion.191) | copy-start | bytes 196612
  113.6 10.5 %copy-start.45 = (bf16[128,768]{1,0:T(8,128)(2,1)S(1)}, bf16[128,768]{1,0:T(8,128)(2,1)}, u32[]{:S(2)}) copy-start(bf16[128,768]{1,0:T(8,128)(2,1)} %param.24) | copy-start | bytes 589828
  115.1 9.0 copy-start.34
  116.7 9.7 %copy-start.4 = (f32[128,1536]{1,0:T(8,128)}, f32[128,1536]{1,0:T(8,128)S(1)}, u32[]{:S(2)}) copy-start(f32[128,1536]{1,0:T(8,128)S(1)} %get-tuple-element.798) | copy-start | bytes 2359300
  124.1 42.8 %copy-start.87 = (f32[768]{0:T(1024)S(1)}, f32[768]{0:T(1024)}, u32[]{:S(2)}) copy-start(f32[768]{0:T(1024)} %get-tuple-element.723) | copy-start | bytes 9220
  126.4 40.5 %copy-start.179 = (f32[128]{0:T(128)}, f32[128]{0:T(128)S(1)}, u32[]{:S(2)}) copy-start(f32[128]{0:T(128)S(1)} %get-tuple-element.841) | copy-start | bytes 1540
  126.4 43.9 %copy-start.20 = (f32[128,768]{1,0:T(8,128)}, f32[128,768]{1,0:T(8,128)S(1)}, u32[]{:S(2)}) copy-start(f32[128,768]{1,0:T(8,128)S(1)} %get-tuple-element.842) | copy-start | bytes 1179652
  126.5 43.9 %copy-start.146 = (f32[128]{0:T(128)}, f32[128]{0:T(128)S(1)}, u32[]{:S(2)}) copy-start(f32[128]{0:T(128)S(1)} %fusion.201) | copy-start | bytes 1540
  171.6 5.4 copy-start.56
  174.1 4.3 collective-permute-start.1
  185.5 54.9 %all-gather.31.cloned.1.call-start = ((), (), s32[]{:S(2)}) async-start(), calls=%async_computation.13 | async-start | bytes 2949120 | tf_op jit(solution)/shard_map/all_gather | solution.py:231
  186.1 98.8 %all-gather.33.cloned.1.call-start = ((), (), s32[]{:S(2)}) async-start(), calls=%async_computation.14 | async-start | bytes 1966080 | tf_op jit(solution)/shard_map/all_gather | solution.py:44
  225.0 55.7 %copy-start = (f32[24,64,128]{2,1,0:T(8,128)}, f32[24,64,128]{2,1,0:T(8,128)S(1)}, u32[]{:S(2)}) copy-start(f32[24,64,128]{2,1,0:T(8,128)S(1)} %get-tuple-element.636) | copy-start | bytes 2359300
  253.0 120.9 %all-gather.35.cloned.1.call-start = ((), (), s32[]{:S(2)}) async-start(), calls=%async_computation.15 | async-start | bytes 1966080 | tf_op jit(solution)/shard_map/all_gather | solution.py:44
  306.8 6.7 copy-start.76
  306.8 6.7 copy-start.157
  308.4 8.1 collective-permute-start.2
  319.7 5.2 copy-start.88
  319.7 5.4 copy-start.29
  319.7 5.4 copy-start.85
  319.7 5.4 copy-start.149
  337.6 71.9 %reduce-scatter.11.cloned.1.call-start = ((), (), s32[]{:S(2)}) async-start(), calls=%async_computation.7 | async-start | bytes 2949120 | tf_op jit(solution)/shard_map/reduce_scatter | solution.py:248
  340.6 88.8 %reduce-scatter.9.cloned.1.call-start = ((), (), s32[]{:S(2)}) async-start(), calls=%async_computation.6 | async-start | bytes 2949120 | tf_op jit(solution)/shard_map/reduce_scatter | solution.py:248
  344.7 139.6 %reduce-scatter.7.cloned.1.call-start = ((), (), s32[]{:S(2)}) async-start(), calls=%async_computation.5 | async-start | bytes 6635520 | tf_op jit(solution)/shard_map/reduce_scatter | solution.py:314
  351.0 187.6 %reduce-scatter.5.cloned.1.call-start = ((), (), s32[]{:S(2)}) async-start(), calls=%async_computation.4 | async-start | bytes 6635520 | tf_op jit(solution)/shard_map/reduce_scatter | solution.py:314
  358.5 7.2 copy-start.16
  393.7 8.2 collective-permute-start.3
  407.3 167.5 %all-reduce.37.cloned.1.call-start = ((), (), s32[]{:S(2)}) async-start(), calls=%async_computation.18 | async-start | bytes 186368 | tf_op jit(solution)/shard_map/psum | solution.py:348
  419.1 409.5 %all-reduce.35.cloned.1.call-start = ((), (), s32[]{:S(2)}) async-start(), calls=%async_computation.17 | async-start | bytes 15335424 | tf_op jit(solution)/shard_map/psum | solution.py:339
  541.6 363.2 %all-reduce.33.cloned.1.call-start = ((), (), s32[]{:S(2)}) async-start(), calls=%async_computation.16 | async-start | bytes 186368 | tf_op jit(solution)/shard_map/psum | solution.py:348
  828.7 5.4 copy-start.64
  828.7 5.4 copy-start.65
  (155 other events, 377.6 us)
Sparse Core Ops, SparseCore 0:
  10.8 41.9 all-gather.20
  68.2 30.1 all-gather.22
  100.0 24.0 all-gather.24
  126.1 40.7 all-gather.26
  185.6 29.2 all-gather.28
  216.3 24.0 all-gather.30
  253.1 19.6 all-gather.32
  337.8 20.4 all-gather.34
  361.3 32.8 reduce-scatter.10
  396.6 32.8 reduce-scatter.8
  432.5 51.7 reduce-scatter.6
  486.8 51.7 reduce-scatter.4
  542.6 32.1 all-reduce.36
  580.4 248.2 all-reduce.34
  832.7 72.0 all-reduce.32
